TPU v7x, 512 devices: a whole 4x4x16 slice. The times are simulated.
512 devices in a mesh: wide: 64 (over z, x), narrow: 8 (over y, core).
Axes of the slice: x: 4, y: 4, z: 16, core: 2. Of those that a mesh axis runs over, the one named last changes fastest.
Arguments:
- integrals: bfloat16 [16384, 65536], P('wide', 'narrow'), may hold values from -0.0625 to 0.0625
- amp_tiles: bfloat16 [8, 786432], P('narrow', 'wide'), may hold values from -6 to 6
- row_orbitals: int32 [16384, 2], P('wide'), may hold values from 0 to 511
- orb_irrep: int32 [512], replicated, may hold values from 0 to 3
- occ_pairs: int32 [96, 2], replicated, may hold values from 0 to 15
- occ_irrep: int32 [16], replicated, may hold values from 0 to 3
Outputs:
- residual: float32 [16384, 96], P(('wide', 'narrow'))
All inputs are finite; a program needn't handle non-finite values.
Results may differ from a plain program's by a relative error of at most 0.0003.
Values may be sent and summed in bfloat16 or wider, within the bound.
A program may use at most 64 MiB of HBM per device.

v0:
```python
import jax
import jax.numpy as jnp
from jax import lax
from jax.sharding import PartitionSpec as P


def lookup_irrep(orbitals, table):
    hits = orbitals[..., None] == jnp.arange(table.shape[0], dtype=jnp.int32)
    return jnp.sum(jnp.where(hits, table, 0), axis=-1)


def shards(integrals, amp_tiles, row_orbitals, orb_irrep, occ_pairs, occ_irrep):
    pair_count = occ_pairs.shape[0]
    column_count = integrals.shape[1]
    row_labels = lookup_irrep(row_orbitals, orb_irrep)
    pair_labels = lookup_irrep(occ_pairs, occ_irrep)
    row_sym = jnp.bitwise_xor(row_labels[:, 0], row_labels[:, 1])
    pair_sym = jnp.bitwise_xor(pair_labels[:, 0], pair_labels[:, 1])
    keep = row_sym[:, None] == pair_sym[None, :]
    gathered = lax.all_gather(amp_tiles, "wide", axis=1, tiled=True)
    amplitudes = gathered.reshape(column_count, pair_count)
    block = jnp.dot(integrals, amplitudes, preferred_element_type=jnp.float32)
    return lax.psum_scatter(
        jnp.where(keep, block, jnp.zeros_like(block)), "narrow", scatter_dimension=0, tiled=True
    )


def solution(mesh):
    in_specs = (P("wide", "narrow"), P("narrow", "wide"), P("wide", None), P(), P(), P())
    out_specs = P(("wide", "narrow"), None)
    return jax.shard_map(shards, mesh=mesh, in_specs=in_specs, out_specs=out_specs, check_vma=False)
```

profile of v0, /device:TPU:4, one launch (start us, length us, event | category | flops | bytes accessed | tf_op | source)
XLA Modules:
  0.0 240.3 jit_solution(9293615291129486285)
XLA Ops:
  6.5 0.0 all-gather.2.cloned.1.call-start
  6.5 0.7 all-gather.2.cloned.1.call-update
  7.3 0.0 reduce-scatter.2.cloned.1.call-start
  7.3 0.8 select_reduce_fusion.1
  8.1 1.0 select_reduce_fusion
  9.1 147.8 %all-gather.2.cloned.1.call-done = bf16[1,786432]{1,0:T(2,128)(2,1)} async-done(((bf16[1,12288]{1,0:T(2,128)(2,1)}), bf16[1,786432]{1,0:T(2,128)(2,1)}) %all-gather.2.cloned.1.call-update) | async-done | bytes 1572880 | tf_op jit(solution)/shard_map/all_gather | solution.py:20
  156.8 34.8 %reduce = bf16[786432]{0:T(1024)(128)(2,1)} reduce(bf16[1,786432]{1,0:T(2,128)(2,1)} %all-gather.2.cloned.1.call-done, bf16[]{:T(256)} %constant.5), dimensions={0}, to_apply=%all_gather.3.reduce_sub_computation | reduce | bytes 3145730 | tf_op jit(solution)/shard_map/all_gather | solution.py:20
  191.6 3.2 %reshape.15 = bf16[8192,96]{1,0:T(8,128)(2,1)S(1)} reshape(bf16[786432]{0:T(1024)(128)(2,1)} %reduce) | data formatting | bytes 3145728 | tf_op jit(solution)/shard_map/reshape | solution.py:21
  194.9 4.1 %convolution_select_fusion = f32[256,96]{1,0:T(8,128)} fusion(bf16[256,8192]{1,0:T(8,128)(2,1)} %param.6, bf16[8192,96]{1,0:T(8,128)(2,1)S(1)} %reshape.15, s32[96]{0:T(128)S(1)} %xor_bitcast_fusion, s32[256]{0:T(256)S(1)} %bitcast.5), kind=kOutput, calls=%fused_computation | convolution fusion | flops 402702336 | bytes 5866880 | tf_op jit(solution)/shard_map/dot_general | solution.py:22
  198.9 0.0 reduce-scatter.2.cloned.1.call-update
  198.9 34.5 %reduce-scatter.2.cloned.1.call-done = f32[32,96]{1,0:T(8,128)} async-done(((f32[256,96]{1,0:T(8,128)}), f32[32,96]{1,0:T(8,128)}) %reduce-scatter.2.cloned.1.call-update) | async-done | bytes 12304 | tf_op jit(solution)/shard_map/reduce_scatter | solution.py:23
  (2 shorter events, 0.0 us)
Async XLA Ops:
  6.5 150.3 %all-gather.2.cloned.1.call-start = ((), (), s32[]{:S(2)}) async-start(), calls=%async_computation.1 | async-start | bytes 3194880 | tf_op jit(solution)/shard_map/all_gather | solution.py:20
  7.3 226.2 %reduce-scatter.2.cloned.1.call-start = ((), (), s32[]{:S(2)}) async-start(), calls=%async_computation.2 | async-start | bytes 147456 | tf_op jit(solution)/shard_map/reduce_scatter | solution.py:23
Sparse Core Ops, SparseCore 0:
  10.3 146.4 all-gather.1
  199.1 34.3 reduce-scatter.1
where the time goes:
time: 241 us; the launch traced here: 240 us
  waiting for transfers between devices  183 us (76%)
  other arithmetic  36.5 us (15%)
  between operations  13.4 us (6%)
  matrix products  4.07 us (2%)
  local copies, waits for them, and re-layouts  3.24 us (1%)
    all_gather x1, waiting for transfers between devices, shards(): gathered = lax.all_gather(amp_tiles, 'wide', axis=1, tiled=True)  148 us
    all_gather x1, other arithmetic, shards(): gathered = lax.all_gather(amp_tiles, 'wide', axis=1, tiled=True)  34.8 us
    reduce_scatter x1, waiting for transfers between devices, shards(): lax.psum_scatter(jnp.where(keep, block, jnp.zeros_like(block)), 'narrow',...  34.5 us
  transfers between devices with their start and end apart: 2, of which 2 were waited for; matrix products, arithmetic and copies ran while one was open for 1% of the time, Pallas kernels for 0%

commit v1 on v0

--- a/solution.py
+++ b/solution.py
@@ -17,7 +17,9 @@
     row_sym = jnp.bitwise_xor(row_labels[:, 0], row_labels[:, 1])
     pair_sym = jnp.bitwise_xor(pair_labels[:, 0], pair_labels[:, 1])
     keep = row_sym[:, None] == pair_sym[None, :]
-    gathered = lax.all_gather(amp_tiles, "wide", axis=1, tiled=True)
+    gathered = jnp.concatenate(
+        lax.all_to_all(jnp.stack([amp_tiles] * lax.axis_size("wide")), "wide", 0, 0), axis=1
+    )
     amplitudes = gathered.reshape(column_count, pair_count)
     block = jnp.dot(integrals, amplitudes, preferred_element_type=jnp.float32)
     return lax.psum_scatter(

time: 241 us -> 189 us (0.78)
  the two profiles are of different devices: /device:TPU:4 before, /device:TPU:2 now
where the time goes in v1:
time: 189 us; the launch traced here: 188 us
  waiting for transfers between devices  107 us (57%)
  other arithmetic  23.4 us (12%)
  local copies, waits for them, and re-layouts  21 us (11%)
  starting transfers between devices  19 us (10%)
  between operations  13.5 us (7%)
  matrix products  4.07 us (2%)
    all_to_all x1, waiting for transfers between devices, shards(): lax.all_to_all(jnp.stack([amp_tiles] * lax.axis_size('wide')), 'wide', 0, 0)  77.1 us
    reduce_scatter x1, waiting for transfers between devices, shards(): lax.psum_scatter(jnp.where(keep, block, jnp.zeros_like(block)), 'narrow',...  29.8 us
    all_to_all x1, starting transfers between devices, shards(): lax.all_to_all(jnp.stack([amp_tiles] * lax.axis_size('wide')), 'wide', 0, 0)  18.9 us
    unnamed x10, local copies, waits for them, and re-layouts  14 us
    another operation x1, other arithmetic, shards(): jnp.stack([amp_tiles] * lax.axis_size('wide'))  11.4 us
    all_to_all x1, other arithmetic, shards(): lax.all_to_all(jnp.stack([amp_tiles] * lax.axis_size('wide')), 'wide', 0, 0)  10.7 us
    dot_general x1, matrix products, shards(): block = jnp.dot(integrals, amplitudes, preferred_element_type=jnp.float32)  4.07 us
  transfers between devices with their start and end apart: 2, of which 2 were waited for; matrix products, arithmetic and copies ran while one was open for 0% of the time, Pallas kernels for 0%

profile of v1, /device:TPU:2, one launch (start us, length us, event | category | flops | bytes accessed | tf_op | source)
XLA Modules:
  0.0 187.9 jit_solution(1524057648933296750)
XLA Ops:
  6.5 0.9 reduce
  7.5 3.0 %stack.2 = bf16[64,1,12288]{2,1,0:T(2,128)(2,1)S(1)} broadcast(bf16[12288]{0:T(1024)(128)(2,1)S(1)} %reduce), dimensions={2} | broadcast | bytes 1597440 | tf_op jit(solution)/shard_map/stack | solution.py:21
  10.5 0.5 broadcast.7
  11.0 11.4 %reduce.2 = bf16[64,12288]{1,0:T(8,128)(2,1)} reduce(bf16[64,1,12288]{2,1,0:T(2,128)(2,1)S(1)} %stack.2, bf16[]{:T(256)} %broadcast.7), dimensions={1}, to_apply=%stack.2.reduce_sub_computation | reduce | bytes 3145730 | tf_op jit(solution)/shard_map/stack | solution.py:21
  22.4 4.9 %reshape.17 = bf16[64,2,6144]{2,1,0:T(2,128)(2,1)} reshape(bf16[64,12288]{1,0:T(8,128)(2,1)} %reduce.2) | data formatting | bytes 3145728
  27.3 0.0 copy-start.2
  27.3 0.0 copy-start.3
  27.3 0.0 copy-start
  27.3 0.0 copy-start.1
  27.3 18.9 %all-to-all-start = ((bf16[64,2,6144]{2,1,0:T(2,128)(2,1)}), bf16[64,2,6144]{2,1,0:T(2,128)(2,1)}, u32[]{:S(2)}, u32[]{:S(2)}) async-start(bf16[64,2,6144]{2,1,0:T(2,128)(2,1)} %reshape.17), calls=%async_computation | async-start | bytes 3145728 | tf_op jit(solution)/shard_map/all_to_all | solution.py:21
  46.3 0.0 reduce-scatter.2.cloned.1.call-start
  46.3 0.0 copy-done.2
  46.3 0.0 copy-done.3
  46.3 0.1 select_reduce_fusion.1
  46.4 0.0 copy-done
  46.4 0.0 copy-done.1
  46.4 0.3 select_reduce_fusion
  46.7 77.1 %all-to-all-done = bf16[64,2,6144]{2,1,0:T(2,128)(2,1)} async-done(((bf16[64,2,6144]{2,1,0:T(2,128)(2,1)}), bf16[64,2,6144]{2,1,0:T(2,128)(2,1)}, u32[]{:S(2)}, u32[]{:S(2)}) %all-to-all-start) | async-done | bytes 1572896 | tf_op jit(solution)/shard_map/all_to_all | solution.py:21
  123.8 9.1 %reshape.18 = bf16[64,1,12288]{2,1,0:T(2,128)(2,1)S(1)} reshape(bf16[64,2,6144]{2,1,0:T(2,128)(2,1)} %all-to-all-done) | data formatting | bytes 3145728
  132.9 10.7 %reduce.1 = bf16[64,12288]{1,0:T(8,128)(2,1)} reduce(bf16[64,1,12288]{2,1,0:T(2,128)(2,1)S(1)} %reshape.18, bf16[]{:T(256)} %constant.5), dimensions={1}, to_apply=%all_to_all.3.reduce_sub_computation | reduce | bytes 3145730 | tf_op jit(solution)/shard_map/all_to_all | solution.py:21
  143.7 3.4 %reshape_reshape.3 = bf16[8192,96]{1,0:T(8,128)(2,1)S(1)} reshape(bf16[64,12288]{1,0:T(8,128)(2,1)} %reduce.1) | data formatting | bytes 3145728 | tf_op jit(solution)/shard_map/reshape;reshape | solution.py:23
  147.1 4.1 %convolution_select_fusion = f32[256,96]{1,0:T(8,128)} fusion(bf16[256,8192]{1,0:T(8,128)(2,1)} %param.6, bf16[8192,96]{1,0:T(8,128)(2,1)S(1)} %reshape_reshape.3, s32[96]{0:T(128)S(1)} %xor_bitcast_fusion, s32[256]{0:T(256)S(1)} %bitcast.5), kind=kOutput, calls=%fused_computation | convolution fusion | flops 402702336 | bytes 5866880 | tf_op jit(solution)/shard_map/dot_general | solution.py:24
  151.2 0.0 reduce-scatter.2.cloned.1.call-update
  151.2 29.8 %reduce-scatter.2.cloned.1.call-done = f32[32,96]{1,0:T(8,128)} async-done(((f32[256,96]{1,0:T(8,128)}), f32[32,96]{1,0:T(8,128)}) %reduce-scatter.2.cloned.1.call-update) | async-done | bytes 12304 | tf_op jit(solution)/shard_map/reduce_scatter | solution.py:25
  (2 shorter events, 0.0 us)
Async XLA Ops:
  27.3 19.0 %copy-start.2 = (s32[96,2]{0,1:T(2,128)S(1)}, s32[96,2]{0,1:T(2,128)}, u32[]{:S(2)}) copy-start(s32[96,2]{0,1:T(2,128)} %param.10) | copy-start | bytes 2308
  27.3 19.0 %copy-start.3 = (s32[16]{0:T(128)S(1)}, s32[16]{0:T(128)}, u32[]{:S(2)}) copy-start(s32[16]{0:T(128)} %param.11) | copy-start | bytes 196
  27.3 19.1 %copy-start = (s32[512]{0:T(512)S(1)}, s32[512]{0:T(512)}, u32[]{:S(2)}) copy-start(s32[512]{0:T(512)} %param.9) | copy-start | bytes 6148
  27.3 19.1 %copy-start.1 = (s32[256,2]{0,1:T(2,128)S(1)}, s32[256,2]{0,1:T(2,128)}, u32[]{:S(2)}) copy-start(s32[256,2]{0,1:T(2,128)} %param.8) | copy-start | bytes 6148
  27.3 96.5 %all-to-all-start = ((bf16[64,2,6144]{2,1,0:T(2,128)(2,1)}), bf16[64,2,6144]{2,1,0:T(2,128)(2,1)}, u32[]{:S(2)}, u32[]{:S(2)}) async-start(bf16[64,2,6144]{2,1,0:T(2,128)(2,1)} %reshape.17), calls=%async_computation | async-start | bytes 3145728 | tf_op jit(solution)/shard_map/all_to_all | solution.py:21
  46.3 134.8 %reduce-scatter.2.cloned.1.call-start = ((), (), s32[]{:S(2)}) async-start(), calls=%async_computation.2 | async-start | bytes 147456 | tf_op jit(solution)/shard_map/reduce_scatter | solution.py:25
Sparse Core Ops, SparseCore 0:
  151.3 29.6 reduce-scatter.1
